TPU v7x, 32 devices: a whole 2x2x4 slice. The times are simulated.
32 devices in a mesh: group: 2 (over y), freq: 4 (over z), shot: 2 (over x), half: 2 (over core).
Axes of the slice: x: 2, y: 2, z: 4, core: 2. Of those that a mesh axis runs over, the one named last changes fastest.
Arguments:
- records: bfloat16 [8, 64, 128, 512], P(('group', 'shot'), 'half', 'freq'), parts along dimension 0, may hold values from -6 to 6
- source_pattern: bfloat16 [8, 64, 128], P(('group', 'shot'), 'half'), parts along dimension 0, may hold values from -6 to 6
- wavelet: float32 [256, 2], replicated, may hold values from -6 to 6
- filters: bfloat16 [2, 2, 13, 13, 256], replicated, may hold values from -0.3125 to 0.3125
- vel_table: float32 [64], replicated, may hold values from 0 to 1
- vel_index: int32 [4, 64, 128], P('group', 'half'), parts along dimension 0, may hold values from 0 to 63
- freq_plan: int32 [4, 6], replicated, may hold values from 0 to 255, as said below
- counts: int32 [4], replicated, may hold values from 1 to 6, 12 in all
Outputs:
- image: float32 [2, 32, 4, 128], P('half', 'freq', 'group'), parts along dimension 2
There are 2 independent parts, one for each index of `group`. A program takes and returns all parts, laid end to end along the dimension named above; an argument that names none is the same for every part. Nothing has to cross between parts.
Inputs may be any that keep to these rules, and one draw needn't show every extreme that they name: `freq_plan`: entries are distinct bins; 0 and 255 both appear. `counts`: they sum to 12; the largest is exactly 6.
All inputs are finite; a program needn't handle non-finite values.
Results may differ from a plain program's by a relative error of at most 0.0069.
Values may be sent and summed in bfloat16 or wider, within the bound.
A program may use at most 64 MiB of HBM per device.

v0:
```python
import functools
import math

import jax
import jax.numpy as jnp
from jax import lax
from jax.experimental import pallas as pl
from jax.experimental.pallas import tpu as pltpu
from jax.sharding import PartitionSpec as P

LANES = 128
SUB = 8
SEG = 16
MESH = pl.DeviceIdType.MESH
FPD = 3


def kernel(
    dims,
    records_any, pattern_any, wavelet_any, filters_any, table_any, index_any, plan_any, counts_any,
    out_ref,
    records_ref, pattern_ref, wavelet_ref, filters_ref, table_ref, index_ref, plan_ref, counts_ref,
    send_ref, recv_ref, taps_ref, bands_ref, stack_ref, field0_ref, field1_ref, part_ref, gather_ref,
    load_sem, a2a_send, a2a_recv, halo_send, halo_recv, red_send, red_recv,
):
    groups, shots_axis, planes, rows, own_cols, taps, nref, depth, samples = dims
    half_taps = taps // 2
    pad = half_taps * SUB
    body_rows = rows * SUB
    freq = lax.axis_index("freq")
    shot = lax.axis_index("shot")
    half = lax.axis_index("half")
    members = groups * shots_axis
    me = freq * shots_axis + shot

    barrier = pltpu.get_barrier_semaphore()
    for step in range(1, members):
        other = lax.rem(me + step, members)
        pl.semaphore_signal(
            barrier, inc=1,
            device_id={"freq": other // shots_axis, "shot": lax.rem(other, shots_axis)},
            device_id_type=MESH,
        )
    pl.semaphore_signal(barrier, inc=1, device_id={"half": 1 - half}, device_id_type=MESH)

    loads = []
    for place, (source, target) in enumerate((
        (counts_any, counts_ref), (plan_any, plan_ref), (records_any, records_ref),
        (filters_any, filters_ref), (wavelet_any, wavelet_ref), (table_any, table_ref),
        (index_any, index_ref), (pattern_any, pattern_ref),
    )):
        copy = pltpu.make_async_copy(source, target, load_sem.at[place])
        copy.start()
        loads.append(copy)
    loads[0].wait()
    loads[1].wait()

    slots = plan_ref.shape[1]

    def bin_of(wanted):
        run = jnp.int32(0)
        start = jnp.int32(0)
        holder = jnp.int32(0)
        for group in range(groups):
            run = run + counts_ref[group]
            past = run <= wanted
            holder = holder + past.astype(jnp.int32)
            start = jnp.where(past, run, start)
        holder = jnp.minimum(holder, groups - 1)
        return plan_ref[holder, jnp.minimum(wanted - start, slots - 1)]

    per_group = SUB // 2
    wave_plane = lax.broadcasted_iota(jnp.int32, (SUB, samples), 0) // 2
    wave_part = lax.broadcasted_iota(jnp.int32, (SUB, samples), 0) % 2
    sample = lax.broadcasted_iota(jnp.int32, (SUB, samples), 1)
    waves = []
    for first in range(0, groups * planes, per_group):
        bins = jnp.zeros((SUB, samples), jnp.int32)
        for plane in range(per_group):
            bins = jnp.where(wave_plane == plane, bin_of(jnp.int32(first + plane)), bins)
        phase = (bins * sample + wave_part * (samples // 4)) & (samples - 1)
        waves.append(phase.astype(jnp.float32) * (2.0 * math.pi / samples))
    waves = jnp.concatenate(waves, axis=0) if len(waves) > 1 else waves[0]
    waves = (jnp.cos(waves) * (1.0 / math.sqrt(samples))).astype(jnp.bfloat16)
    table_rows = groups * planes * SUB
    spread_row = lax.broadcasted_iota(jnp.int32, (table_rows, waves.shape[0]), 0)
    spread_col = lax.broadcasted_iota(jnp.int32, (table_rows, waves.shape[0]), 1)
    spread_to = (spread_row // SUB) * 2 + (spread_row % SUB) // (SUB // 2)
    spread_hot = (spread_col == spread_to).astype(jnp.float32).astype(jnp.bfloat16)
    dft = jnp.dot(spread_hot, waves, preferred_element_type=jnp.float32).astype(jnp.bfloat16)

    sub_row = lax.broadcasted_iota(jnp.int32, (SUB, LANES), 0)
    odd_shot = (sub_row & 1) == 1
    second = (sub_row & 2) == 2
    upper = sub_row >= SUB // 2

    half_lanes = rows * own_cols
    loads[2].wait()
    spectra = []
    for index in range(2):
        block = records_ref[index * half_lanes:(index + 1) * half_lanes, :]
        spectra.append(
            lax.dot_general(dft, block, (((1,), (1,)), ((), ())), preferred_element_type=jnp.float32)
        )
    strips = half_lanes // LANES
    pairs = 2 if strips % 2 == 0 else 1
    packs = strips // pairs
    for holder in range(groups):
        for plane in range(planes):
            pieces = []
            base = (holder * planes + plane) * SUB
            for pack in range(packs):
                chosen = []
                for pair in range(pairs):
                    at = (pack * pairs + pair) * LANES
                    chosen.append(
                        jnp.where(
                            odd_shot,
                            spectra[1][base:base + SUB, at:at + LANES],
                            spectra[0][base:base + SUB, at:at + LANES],
                        )
                    )
                pieces.append(chosen[0] if pairs == 1 else jnp.where(second, chosen[1], chosen[0]))
            piece = jnp.concatenate(pieces, axis=0) if packs > 1 else pieces[0]
            send_ref[holder, plane] = piece.astype(jnp.bfloat16)
    recv_ref[freq] = send_ref[freq]

    pl.semaphore_wait(barrier, members)

    exchanges = []
    for plane in range(planes):
        arriving = []
        for step in range(1, groups):
            other = lax.rem(freq + step, groups)
            copy = pltpu.make_async_remote_copy(
                src_ref=send_ref.at[other, plane],
                dst_ref=recv_ref.at[freq, plane],
                send_sem=a2a_send.at[plane, step],
                recv_sem=a2a_recv.at[plane, step],
                device_id={"freq": other},
                device_id_type=MESH,
            )
            copy.start()
            arriving.append(copy)
        exchanges.append(arriving)

    bin_total = taps_ref.shape[1]
    own_bins = [bin_of(freq * planes + plane) for plane in range(planes)]
    segments = nref * taps
    taps_ref[...] = jnp.zeros_like(taps_ref)
    for copy in loads[3:]:
        copy.wait()
    for segment in range(segments):
        for tap in range(taps):
            at = segment * 2 * SEG + 2 * tap
            taps_ref[at:at + 2, :] = filters_ref[segment, tap]
    bin_lane = lax.broadcasted_iota(jnp.int32, (SUB, bin_total), 1)
    bin_row = lax.broadcasted_iota(jnp.int32, (SUB, bin_total), 0)
    wanted_bin = jnp.full((SUB, bin_total), -1, jnp.int32)
    for plane in range(planes):
        wanted_bin = jnp.where(bin_row == plane, own_bins[plane], wanted_bin)
    bin_hot = (wanted_bin == bin_lane).astype(jnp.float32).astype(jnp.bfloat16)
    picked = lax.dot_general(
        bin_hot, taps_ref[...], (((1,), (1,)), ((), ())), preferred_element_type=jnp.float32
    ).astype(jnp.bfloat16)
    lane_in = lax.broadcasted_iota(jnp.int32, (LANES, LANES), 0)
    lane_out = lax.broadcasted_iota(jnp.int32, (LANES, LANES), 1)
    turn = (
        (lane_in // (2 * SEG) == lane_out // (2 * SEG))
        & (lane_in % 2 == (lane_out % (2 * SEG)) // SEG)
        & ((lane_in % (2 * SEG)) // 2 + lane_out % SEG == taps - 1)
    ).astype(jnp.float32).astype(jnp.bfloat16)
    per_tile = LANES // SEG
    turned = []
    for at in range(0, segments * 2 * SEG, LANES):
        width = min(LANES, segments * 2 * SEG - at)
        turned.append(
            jnp.dot(
                picked[:, at:at + width], turn[:width, :], preferred_element_type=jnp.float32
            )
        )
    in_band = (lane_out - lane_in + half_taps >= 0) & (lane_out - lane_in + half_taps < taps)
    for line in range(2 * segments):
        shift = (-(half_taps + (line % per_tile) * SEG)) % LANES
        placed = pltpu.roll(turned[line // per_tile], shift, 1)
        segment = line // 2
        tap_row = segment % taps
        side = (segment // taps) * 2 + line % 2
        for plane in range(planes):
            wide = jnp.broadcast_to(placed[plane:plane + 1, :], (LANES, LANES))
            rolled = pltpu.roll(wide, 0, 1, stride=1, stride_axis=0)
            bands_ref[
                plane, tap_row * LANES:(tap_row + 1) * LANES, side * LANES:(side + 1) * LANES
            ] = jnp.where(in_band, rolled, 0.0).astype(jnp.bfloat16)

    blends = []
    for level in range(depth):
        classes = index_ref[level]
        weight = jnp.zeros(classes.shape, jnp.float32)
        for entry in range(table_ref.shape[0]):
            weight = jnp.where(classes == entry, table_ref[entry], weight)
        blends.append(weight)

    outer = pl.multiple_of(half * (body_rows + pad), SUB)
    for plane in range(planes):
        field0_ref[plane, pl.ds(outer, pad), :] = jnp.zeros((pad, LANES), jnp.float32)
        field1_ref[plane, pl.ds(outer, pad), :] = jnp.zeros((pad, LANES), jnp.float32)
    pattern = [pattern_ref[index].astype(jnp.float32) for index in range(2)]
    wave_lane = lax.broadcasted_iota(jnp.int32, wavelet_ref.shape, 1)
    gains = []
    for plane in range(planes):
        gain = jnp.sum(
            jnp.where(wave_lane == own_bins[plane], wavelet_ref[...], 0.0), axis=1, keepdims=True
        )
        gains.append(
            jnp.where(
                upper,
                jnp.broadcast_to(gain[1:2, :], (SUB, LANES)),
                jnp.broadcast_to(gain[0:1, :], (SUB, LANES)),
            )
        )

    inner = pl.multiple_of(body_rows - half * (body_rows - pad), SUB)
    target = pl.multiple_of(half * (body_rows + pad), SUB)

    def swap(level, plane):
        field_ref = field0_ref if level == 0 else field1_ref
        copy = pltpu.make_async_remote_copy(
            src_ref=field_ref.at[plane, pl.ds(inner, pad), :],
            dst_ref=field_ref.at[plane, pl.ds(target, pad), :],
            send_sem=halo_send.at[level, plane],
            recv_sem=halo_recv.at[level, plane],
            device_id={"half": 1 - half},
            device_id_type=MESH,
        )
        copy.start()
        return copy

    lane = lax.broadcasted_iota(jnp.int32, (packs * SUB, LANES), 1) // own_cols
    strip_rows = LANES // own_cols

    def assemble(plane):
        for copy in exchanges[plane]:
            copy.wait()
        blocks = [recv_ref[group, plane].astype(jnp.float32) for group in range(groups)]
        for low in range(strip_rows):
            merged = jnp.zeros((packs * SUB, LANES), jnp.float32)
            for group in range(groups):
                shift = ((group - low) * own_cols) % LANES
                moved = blocks[group] if shift == 0 else pltpu.roll(blocks[group], shift, 1)
                merged = jnp.where(lane == group, moved, merged)
            for pack in range(packs):
                value = merged[pack * SUB:(pack + 1) * SUB, :]
                for pair in range(pairs):
                    row = (pack * pairs + pair) * strip_rows + low
                    receiver = value
                    if pairs == 2 and pair == 0:
                        receiver = pltpu.roll(value, 2, 0)
                    source = jnp.where(
                        odd_shot, pattern[1][row:row + 1, :], pattern[0][row:row + 1, :]
                    ) * gains[plane]
                    source = source.astype(jnp.bfloat16).astype(jnp.float32)
                    field0_ref[plane, pad + row * SUB:pad + (row + 1) * SUB, :] = jnp.where(
                        second, receiver, source
                    )
        return swap(0, plane)

    row3 = lax.broadcasted_iota(jnp.int32, (rows, SUB, LANES), 1)
    sign = jnp.where(row3 >= SUB // 2, 1.0, -1.0)
    image_row = (row3 & 2) == 0
    share = rows // groups

    def extrapolate(level, plane):
        field_ref = field0_ref if level == 0 else field1_ref
        for tap_row in range(taps):
            stack_ref[:, tap_row * LANES:(tap_row + 1) * LANES] = field_ref[
                plane, tap_row * SUB:tap_row * SUB + body_rows, :
            ].astype(jnp.bfloat16)
        sides = []
        for side in range(nref):
            both = jnp.dot(
                stack_ref[...],
                bands_ref[plane, :, 2 * side * LANES:2 * (side + 1) * LANES],
                preferred_element_type=jnp.float32,
            )
            direct = both[:, :LANES].reshape(rows, SUB, LANES)
            crossed = both[:, LANES:].reshape(rows, SUB, LANES)
            sides.append(direct + sign * pltpu.roll(crossed, SUB // 2, 1))
        value = sides[0] + blends[level][:, None, :] * (sides[1] - sides[0])
        value = value.astype(jnp.bfloat16).astype(jnp.float32)
        copy = None
        if level + 1 < depth:
            field1_ref[plane, pad:pad + body_rows, :] = value.reshape(body_rows, LANES)
            copy = swap(level + 1, plane)
        return value * pltpu.roll(value, SUB - 2, 1), copy

    halos = {}
    ahead = min(2, planes)
    for plane in range(ahead):
        halos[plane] = assemble(plane)
    reductions = []
    for level in range(depth):
        total = jnp.zeros((rows, SUB, LANES), jnp.float32)
        following = {}
        for plane in range(planes):
            halos[plane].wait()
            term, following[plane] = extrapolate(level, plane)
            total = total + term
            if level == 0 and plane + ahead < planes:
                halos[plane + ahead] = assemble(plane + ahead)
        halos = following
        image = jnp.sum(jnp.where(image_row, total, 0.0), axis=1)
        part_ref[:, level] = image.reshape(groups, share, LANES)
        for step in range(1, members):
            other = lax.rem(me + step, members)
            copy = pltpu.make_async_remote_copy(
                src_ref=part_ref.at[other // shots_axis, level],
                dst_ref=gather_ref.at[me, level],
                send_sem=red_send.at[level, step],
                recv_sem=red_recv.at[level, step],
                device_id={"freq": other // shots_axis, "shot": lax.rem(other, shots_axis)},
                device_id_type=MESH,
            )
            copy.start()
            reductions.append(copy)
    gather_ref[me] = part_ref[freq]
    for copy in reductions:
        copy.wait()
    result = gather_ref[0]
    for index in range(1, members):
        result = result + gather_ref[index]
    for level in range(depth):
        out_ref[0, :, level, :] = result[level]


def body(records, source_pattern, wavelet, filters, vel_table, vel_index, freq_plan, counts):
    groups = lax.axis_size("freq")
    shots_axis = lax.axis_size("shot")
    shot_dev, rows, own_cols, samples = records.shape
    cols = source_pattern.shape[2]
    nref, _, taps, _, bin_total = filters.shape
    depth = vel_index.shape[0]
    planes = FPD
    lines = nref * 2 * taps
    members = groups * shots_axis
    scale = 1.0 / math.sqrt(planes * groups * shot_dev * shots_axis)
    dims = (groups, shots_axis, planes, rows, own_cols, taps, nref, depth, samples)
    strips = rows * own_cols // LANES
    packs = strips // 2 if strips % 2 == 0 else strips
    field_rows = (rows + 2 * (taps // 2)) * SUB
    share = rows // groups
    vmem = pl.BlockSpec(memory_space=pltpu.VMEM)
    anywhere = pl.BlockSpec(memory_space=pl.ANY)
    arguments = (
        records.reshape(shot_dev * rows * own_cols, samples),
        source_pattern,
        wavelet.T,
        filters.transpose(0, 2, 3, 1, 4).reshape(nref * taps, taps, 2, bin_total),
        vel_table,
        vel_index,
        freq_plan,
        counts,
    )
    scalars = (4, 6, 7)
    image = pl.pallas_call(
        functools.partial(kernel, dims),
        out_shape=jax.ShapeDtypeStruct((1, share, depth, cols), jnp.float32),
        in_specs=[anywhere] * len(arguments),
        out_specs=vmem,
        scratch_shapes=[
            (pltpu.SMEM if place in scalars else pltpu.VMEM)(array.shape, array.dtype)
            for place, array in enumerate(arguments)
        ] + [
            pltpu.VMEM((groups, planes, packs * SUB, LANES), jnp.bfloat16),
            pltpu.VMEM((groups, planes, packs * SUB, LANES), jnp.bfloat16),
            pltpu.VMEM((lines * SEG, bin_total), jnp.bfloat16),
            pltpu.VMEM((planes, taps * LANES, nref * 2 * LANES), jnp.bfloat16),
            pltpu.VMEM((rows * SUB, taps * LANES), jnp.bfloat16),
            pltpu.VMEM((planes, field_rows, LANES), jnp.float32),
            pltpu.VMEM((planes, field_rows, LANES), jnp.float32),
            pltpu.VMEM((groups, depth, share, LANES), jnp.float32),
            pltpu.VMEM((members, depth, share, LANES), jnp.float32),
            pltpu.SemaphoreType.DMA((len(arguments),)),
            pltpu.SemaphoreType.DMA((planes, groups)),
            pltpu.SemaphoreType.DMA((planes, groups)),
            pltpu.SemaphoreType.DMA((depth, planes)),
            pltpu.SemaphoreType.DMA((depth, planes)),
            pltpu.SemaphoreType.DMA((depth, members)),
            pltpu.SemaphoreType.DMA((depth, members)),
        ],
        compiler_params=pltpu.CompilerParams(
            collective_id=0, has_side_effects=True, vmem_limit_bytes=60 << 20
        ),
    )(*arguments)
    return image * scale


def solution(mesh):
    return jax.shard_map(
        body,
        mesh=mesh,
        in_specs=(
            P(("group", "shot"), "half", "freq", None),
            P(("group", "shot"), "half", None),
            P(),
            P(),
            P(),
            P("group", "half", None),
            P(),
            P(),
        ),
        out_specs=P("half", "freq", "group", None),
        check_vma=False,
    )
```

profile of v0, /device:TPU:0, one launch (start us, length us, event | category | flops | bytes accessed | tf_op | source)
XLA Modules:
  0.0 23.5 jit_solution(4768432440552594354)
XLA Ops:
  0.0 22.2 %shard_map.82 = f32[1,8,2,128]{3,2,1,0:T(2,128)} custom-call(bf16[2048,512]{1,0:T(8,128)(2,1)} %bitcast.5, bf16[2,32,128]{2,1,0:T(8,128)(2,1)} %pattern_any.1, f32[2,256]{1,0:T(2,128)} %bitcast.7, bf16[26,13,2,256]{3,2,1,0:T(2,128)(2,1)} %bitcast.6, f32[64]{0:T(128)} %table_any.1, s32[2,32,128]{2,1,0:T(8,128)} %index_any.1, s32[4,6]{1,0:T(4,128)} %plan_any.1, ...), custom_call_target="tpu_custom_call" | custom-call | tf_op jit(solution)/shard_map/pallas_call | solution.py:365
  22.2 1.3 %broadcast_multiply_fusion = f32[1,8,2,128]{3,2,1,0:T(2,128)} fusion(f32[1,8,2,128]{3,2,1,0:T(2,128)} %shard_map.82), kind=kLoop, calls=%fused_computation | loop fusion | flops 2048 | bytes 16384 | tf_op jit(solution)/shard_map/mul | solution.py:395
where the time goes:
time: 23.7 us; the launch traced here: 23.5 us
  Pallas kernels  22.2 us (94%)
  other arithmetic  1.3 us (5%)
    pallas_call x1, Pallas kernels, body(): pl.pallas_call(functools.partial(kernel, dims), out_shape=jax.ShapeDtypeS...  22.2 us
    mul x1, other arithmetic, body(): return image * scale  1.3 us

commit v1 on v0

--- a/solution.py
+++ b/solution.py
@@ -350,7 +350,7 @@
     field_rows = (rows + 2 * (taps // 2)) * SUB
     share = rows // groups
     vmem = pl.BlockSpec(memory_space=pltpu.VMEM)
-    anywhere = pl.BlockSpec(memory_space=pl.ANY)
+    anywhere = pl.BlockSpec(memory_space=pltpu.HBM)
     arguments = (
         records.reshape(shot_dev * rows * own_cols, samples),
         source_pattern,
@@ -361,6 +361,7 @@
         freq_plan,
         counts,
     )
+    arguments = tuple(pltpu.with_memory_space_constraint(a, pltpu.HBM) for a in arguments)
     scalars = (4, 6, 7)
     image = pl.pallas_call(
         functools.partial(kernel, dims),
@@ -389,7 +390,7 @@
             pltpu.SemaphoreType.DMA((depth, members)),
         ],
         compiler_params=pltpu.CompilerParams(
-            collective_id=0, has_side_effects=True, vmem_limit_bytes=60 << 20
+            collective_id=0, has_side_effects=True, vmem_limit_bytes=24 << 20
         ),
     )(*arguments)
     return image * scale

time: 23.7 us -> 22.3 us (0.941)
  other arithmetic: 1.3 us -> 0.6 us
  Pallas kernels: 22.2 us -> 21.6 us
    mul x1, other arithmetic: 1.3 us -> 0.6 us  [body(): return image * scale]
    pallas_call x1, Pallas kernels: 22.2 us -> 21.6 us  [body(): pl.pallas_call(functools.partial(kernel, dims), out_shape=jax.ShapeDtypeS...]
where the time goes in v1:
time: 22.3 us; the launch traced here: 22.2 us
  Pallas kernels  21.6 us (97%)
  other arithmetic  0.6 us (3%)
    pallas_call x1, Pallas kernels, body(): pl.pallas_call(functools.partial(kernel, dims), out_shape=jax.ShapeDtypeS...  21.6 us
    mul x1, other arithmetic, body(): return image * scale  0.6 us

profile of v1, /device:TPU:0, one launch (start us, length us, event | category | flops | bytes accessed | tf_op | source)
XLA Modules:
  0.0 22.2 jit_solution(812235791893227872)
XLA Ops:
  0.0 21.6 %shard_map.82 = f32[1,8,2,128]{3,2,1,0:T(2,128)S(1)} custom-call(bf16[2048,512]{1,0:T(8,128)(2,1)} %bitcast.5, bf16[2,32,128]{2,1,0:T(8,128)(2,1)} %pattern_any.1, f32[2,256]{1,0:T(2,128)} %bitcast.7, bf16[26,13,2,256]{3,2,1,0:T(2,128)(2,1)} %bitcast.6, f32[64]{0:T(128)} %table_any.1, s32[2,32,128]{2,1,0:T(8,128)} %index_any.1, s32[4,6]{1,0:T(4,128)} %plan_any.1, ...), custom_call_target="tpu_custom_call" | custom-call | tf_op jit(solution)/shard_map/pallas_call | solution.py:366
  21.6 0.6 %broadcast_multiply_fusion = f32[1,8,2,128]{3,2,1,0:T(2,128)} fusion(f32[1,8,2,128]{3,2,1,0:T(2,128)S(1)} %shard_map.82), kind=kLoop, calls=%fused_computation | loop fusion | flops 2048 | bytes 16384 | tf_op jit(solution)/shard_map/mul | solution.py:396

commit v2 on v1

--- a/solution.py
+++ b/solution.py
@@ -11,6 +11,7 @@
 LANES = 128
 SUB = 8
 SEG = 16
+SLOT = 32
 MESH = pl.DeviceIdType.MESH
 FPD = 3
 
@@ -20,13 +21,15 @@
     records_any, pattern_any, wavelet_any, filters_any, table_any, index_any, plan_any, counts_any,
     out_ref,
     records_ref, pattern_ref, wavelet_ref, filters_ref, table_ref, index_ref, plan_ref, counts_ref,
-    send_ref, recv_ref, taps_ref, bands_ref, stack_ref, field0_ref, field1_ref, part_ref, gather_ref,
-    load_sem, a2a_send, a2a_recv, halo_send, halo_recv, red_send, red_recv,
+    send_ref, recv_ref, edge_ref, edges_ref, beside_ref, taps_ref, lines_ref, bands_ref, stack_ref, field0_ref, field1_ref,
+    part_ref, gather_ref,
+    load_sem, a2a_send, a2a_recv, edge_send, edge_recv, beside_send, beside_recv, halo_send, halo_recv, red_send, red_recv,
 ):
-    groups, shots_axis, planes, rows, own_cols, taps, nref, depth, samples = dims
+    groups, shots_axis, planes, rows, own_cols, taps, nref, depth, samples, packs, pairs, edge_packs, margin = dims
     half_taps = taps // 2
     pad = half_taps * SUB
     body_rows = rows * SUB
+    slack = margin * SUB
     freq = lax.axis_index("freq")
     shot = lax.axis_index("shot")
     half = lax.axis_index("half")
@@ -34,13 +37,13 @@
     me = freq * shots_axis + shot
 
     barrier = pltpu.get_barrier_semaphore()
-    for step in range(1, members):
-        other = lax.rem(me + step, members)
-        pl.semaphore_signal(
-            barrier, inc=1,
-            device_id={"freq": other // shots_axis, "shot": lax.rem(other, shots_axis)},
-            device_id_type=MESH,
-        )
+    for step in range(1, groups):
+        other = lax.rem(freq + step, groups)
+        pl.semaphore_signal(barrier, inc=1, device_id={"freq": other}, device_id_type=MESH)
+        pl.semaphore_signal(barrier, inc=1, device_id={"freq": other, "half": 1 - half}, device_id_type=MESH)
+    for step in range(1, shots_axis):
+        other = lax.rem(shot + step, shots_axis)
+        pl.semaphore_signal(barrier, inc=1, device_id={"shot": other}, device_id_type=MESH)
     pl.semaphore_signal(barrier, inc=1, device_id={"half": 1 - half}, device_id_type=MESH)
 
     loads = []
@@ -102,9 +105,6 @@
         spectra.append(
             lax.dot_general(dft, block, (((1,), (1,)), ((), ())), preferred_element_type=jnp.float32)
         )
-    strips = half_lanes // LANES
-    pairs = 2 if strips % 2 == 0 else 1
-    packs = strips // pairs
     for holder in range(groups):
         for plane in range(planes):
             pieces = []
@@ -123,9 +123,13 @@
                 pieces.append(chosen[0] if pairs == 1 else jnp.where(second, chosen[1], chosen[0]))
             piece = jnp.concatenate(pieces, axis=0) if packs > 1 else pieces[0]
             send_ref[holder, plane] = piece.astype(jnp.bfloat16)
+            border = jnp.where(half == 0, piece[(packs - edge_packs) * SUB:, :], piece[:edge_packs * SUB, :])
+            edge_ref[holder, plane] = border.astype(jnp.bfloat16)
     recv_ref[freq] = send_ref[freq]
 
-    pl.semaphore_wait(barrier, members)
+    pl.semaphore_wait(barrier, 2 * (groups - 1) + shots_axis)
+    for copy in loads[3:]:
+        copy.wait()
 
     exchanges = []
     for plane in range(planes):
@@ -142,56 +146,83 @@
             )
             copy.start()
             arriving.append(copy)
+        for step in range(groups):
+            other = lax.rem(freq + step, groups)
+            copy = pltpu.make_async_remote_copy(
+                src_ref=edge_ref.at[other, plane],
+                dst_ref=edges_ref.at[freq, plane],
+                send_sem=edge_send.at[plane, step],
+                recv_sem=edge_recv.at[plane, step],
+                device_id={"freq": other, "half": 1 - half},
+                device_id_type=MESH,
+            )
+            copy.start()
+            arriving.append(copy)
         exchanges.append(arriving)
+    beside = pltpu.make_async_remote_copy(
+        src_ref=pattern_ref,
+        dst_ref=beside_ref,
+        send_sem=beside_send.at[0],
+        recv_sem=beside_recv.at[0],
+        device_id={"half": 1 - half},
+        device_id_type=MESH,
+    )
+    beside.start()
 
     bin_total = taps_ref.shape[1]
     own_bins = [bin_of(freq * planes + plane) for plane in range(planes)]
     segments = nref * taps
     taps_ref[...] = jnp.zeros_like(taps_ref)
-    for copy in loads[3:]:
-        copy.wait()
     for segment in range(segments):
         for tap in range(taps):
             at = segment * 2 * SEG + 2 * tap
             taps_ref[at:at + 2, :] = filters_ref[segment, tap]
-    bin_lane = lax.broadcasted_iota(jnp.int32, (SUB, bin_total), 1)
-    bin_row = lax.broadcasted_iota(jnp.int32, (SUB, bin_total), 0)
-    wanted_bin = jnp.full((SUB, bin_total), -1, jnp.int32)
+    bin_lane = lax.broadcasted_iota(jnp.int32, (planes * SUB, bin_total), 1)
+    bin_row = lax.broadcasted_iota(jnp.int32, (planes * SUB, bin_total), 0) // SUB
+    wanted_bin = jnp.full((planes * SUB, bin_total), -1, jnp.int32)
     for plane in range(planes):
         wanted_bin = jnp.where(bin_row == plane, own_bins[plane], wanted_bin)
     bin_hot = (wanted_bin == bin_lane).astype(jnp.float32).astype(jnp.bfloat16)
     picked = lax.dot_general(
         bin_hot, taps_ref[...], (((1,), (1,)), ((), ())), preferred_element_type=jnp.float32
     ).astype(jnp.bfloat16)
-    lane_in = lax.broadcasted_iota(jnp.int32, (LANES, LANES), 0)
-    lane_out = lax.broadcasted_iota(jnp.int32, (LANES, LANES), 1)
+    per_tile = LANES // SLOT
+    pick_lane = lax.broadcasted_iota(jnp.int32, (LANES, 2 * LANES), 0)
+    turn_lane = lax.broadcasted_iota(jnp.int32, (LANES, 2 * LANES), 1)
     turn = (
-        (lane_in // (2 * SEG) == lane_out // (2 * SEG))
-        & (lane_in % 2 == (lane_out % (2 * SEG)) // SEG)
-        & ((lane_in % (2 * SEG)) // 2 + lane_out % SEG == taps - 1)
+        (pick_lane // (2 * SEG) == turn_lane // (2 * SLOT))
+        & (pick_lane % 2 == (turn_lane // SLOT) % 2)
+        & ((pick_lane % (2 * SEG)) // 2 + turn_lane % SLOT == taps - 1)
     ).astype(jnp.float32).astype(jnp.bfloat16)
-    per_tile = LANES // SEG
-    turned = []
     for at in range(0, segments * 2 * SEG, LANES):
         width = min(LANES, segments * 2 * SEG - at)
-        turned.append(
-            jnp.dot(
-                picked[:, at:at + width], turn[:width, :], preferred_element_type=jnp.float32
-            )
-        )
-    in_band = (lane_out - lane_in + half_taps >= 0) & (lane_out - lane_in + half_taps < taps)
-    for line in range(2 * segments):
-        shift = (-(half_taps + (line % per_tile) * SEG)) % LANES
-        placed = pltpu.roll(turned[line // per_tile], shift, 1)
-        segment = line // 2
-        tap_row = segment % taps
-        side = (segment // taps) * 2 + line % 2
+        turned = jnp.dot(picked[:, at:at + width], turn[:width, :], preferred_element_type=jnp.float32)
+        first = at // SEG
+        for line in range(first, min(first + 2 * per_tile, 2 * segments), 2):
+            place = (line - first) * SLOT
+            for plane in range(planes):
+                base = turned[plane * SUB:(plane + 1) * SUB, place // LANES * LANES:place // LANES * LANES + LANES]
+                shift = -(place % LANES) % LANES
+                own = pltpu.roll(base, shift, 1, stride=1, stride_axis=0)
+                after = pltpu.roll(base, (shift - SLOT) % LANES, 1, stride=1, stride_axis=0)
+                lines_ref[plane, line * SUB:(line + 2) * SUB, :] = jnp.concatenate([own, after], axis=0).astype(jnp.bfloat16)
+    spread = lax.broadcasted_iota(jnp.int32, (SLOT, LANES), 1) - lax.broadcasted_iota(jnp.int32, (SLOT, LANES), 0)
+    rest = jnp.zeros((LANES - SLOT, 2 * LANES), jnp.bfloat16)
+    placed = lines_ref[...].reshape(planes * 2 * segments * SUB, LANES)
+    for first in range(0, LANES, 2 * SUB):
+        moves = jnp.concatenate(
+            [(spread == first + more - half_taps).astype(jnp.float32) for more in (0, SUB)], axis=1
+        ).astype(jnp.bfloat16)
+        block = jnp.dot(placed, jnp.concatenate([moves, rest], axis=0), preferred_element_type=jnp.float32)
         for plane in range(planes):
-            wide = jnp.broadcast_to(placed[plane:plane + 1, :], (LANES, LANES))
-            rolled = pltpu.roll(wide, 0, 1, stride=1, stride_axis=0)
-            bands_ref[
-                plane, tap_row * LANES:(tap_row + 1) * LANES, side * LANES:(side + 1) * LANES
-            ] = jnp.where(in_band, rolled, 0.0).astype(jnp.bfloat16)
+            for line in range(2 * segments):
+                segment = line // 2
+                at = (segment % taps) * LANES + first
+                side = (segment // taps) * 2 + line % 2
+                start = (plane * 2 * segments + line) * SUB
+                bands_ref[plane, at:at + 2 * SUB, side * LANES:(side + 1) * LANES] = jnp.concatenate(
+                    [block[start:start + SUB, :LANES], block[start:start + SUB, LANES:]], axis=0
+                ).astype(jnp.bfloat16)
 
     blends = []
     for level in range(depth):
@@ -202,8 +233,9 @@
         blends.append(weight)
 
     outer = pl.multiple_of(half * (body_rows + pad), SUB)
+    outer0 = pl.multiple_of(slack + half * (body_rows + pad), SUB)
     for plane in range(planes):
-        field0_ref[plane, pl.ds(outer, pad), :] = jnp.zeros((pad, LANES), jnp.float32)
+        field0_ref[plane, pl.ds(outer0, pad), :] = jnp.zeros((pad, LANES), jnp.float32)
         field1_ref[plane, pl.ds(outer, pad), :] = jnp.zeros((pad, LANES), jnp.float32)
     pattern = [pattern_ref[index].astype(jnp.float32) for index in range(2)]
     wave_lane = lax.broadcasted_iota(jnp.int32, wavelet_ref.shape, 1)
@@ -224,32 +256,38 @@
     target = pl.multiple_of(half * (body_rows + pad), SUB)
 
     def swap(level, plane):
-        field_ref = field0_ref if level == 0 else field1_ref
+        field_ref = field1_ref
         copy = pltpu.make_async_remote_copy(
             src_ref=field_ref.at[plane, pl.ds(inner, pad), :],
             dst_ref=field_ref.at[plane, pl.ds(target, pad), :],
-            send_sem=halo_send.at[level, plane],
-            recv_sem=halo_recv.at[level, plane],
+            send_sem=halo_send.at[level - 1, plane],
+            recv_sem=halo_recv.at[level - 1, plane],
             device_id={"half": 1 - half},
             device_id_type=MESH,
         )
         copy.start()
         return copy
 
-    lane = lax.broadcasted_iota(jnp.int32, (packs * SUB, LANES), 1) // own_cols
     strip_rows = LANES // own_cols
-
-    def assemble(plane):
-        for copy in exchanges[plane]:
-            copy.wait()
-        blocks = [recv_ref[group, plane].astype(jnp.float32) for group in range(groups)]
+    edge_rows = edge_packs * pairs * strip_rows
+    edge_at = pl.multiple_of(
+        jnp.where(half == 0, slack + pad + body_rows, slack + pad - edge_rows * SUB), SUB
+    )
+    beside.wait()
+    besides = []
+    for index in range(2):
+        other_half = beside_ref[index].astype(jnp.float32)
+        besides.append(jnp.where(half == 0, other_half[:edge_rows, :], other_half[rows - edge_rows:, :]))
+
+    def unfold(blocks, count, patterns, plane, put):
+        lane = lax.broadcasted_iota(jnp.int32, (count * SUB, LANES), 1) // own_cols
         for low in range(strip_rows):
-            merged = jnp.zeros((packs * SUB, LANES), jnp.float32)
+            merged = jnp.zeros((count * SUB, LANES), jnp.float32)
             for group in range(groups):
                 shift = ((group - low) * own_cols) % LANES
                 moved = blocks[group] if shift == 0 else pltpu.roll(blocks[group], shift, 1)
                 merged = jnp.where(lane == group, moved, merged)
-            for pack in range(packs):
+            for pack in range(count):
                 value = merged[pack * SUB:(pack + 1) * SUB, :]
                 for pair in range(pairs):
                     row = (pack * pairs + pair) * strip_rows + low
@@ -257,13 +295,24 @@
                     if pairs == 2 and pair == 0:
                         receiver = pltpu.roll(value, 2, 0)
                     source = jnp.where(
-                        odd_shot, pattern[1][row:row + 1, :], pattern[0][row:row + 1, :]
+                        odd_shot, patterns[1][row:row + 1, :], patterns[0][row:row + 1, :]
                     ) * gains[plane]
                     source = source.astype(jnp.bfloat16).astype(jnp.float32)
-                    field0_ref[plane, pad + row * SUB:pad + (row + 1) * SUB, :] = jnp.where(
-                        second, receiver, source
-                    )
-        return swap(0, plane)
+                    put(row, jnp.where(second, receiver, source))
+
+    def assemble(plane):
+        for copy in exchanges[plane]:
+            copy.wait()
+
+        def put_body(row, value):
+            at = slack + pad + row * SUB
+            field0_ref[plane, at:at + SUB, :] = value
+
+        def put_edge(row, value):
+            field0_ref[plane, pl.ds(pl.multiple_of(edge_at + row * SUB, SUB), SUB), :] = value
+
+        unfold([recv_ref[group, plane].astype(jnp.float32) for group in range(groups)], packs, pattern, plane, put_body)
+        unfold([edges_ref[group, plane].astype(jnp.float32) for group in range(groups)], edge_packs, besides, plane, put_edge)
 
     row3 = lax.broadcasted_iota(jnp.int32, (rows, SUB, LANES), 1)
     sign = jnp.where(row3 >= SUB // 2, 1.0, -1.0)
@@ -271,10 +320,11 @@
     share = rows // groups
 
     def extrapolate(level, plane):
-        field_ref = field0_ref if level == 0 else field1_ref
+        field_ref, start = (field0_ref, slack) if level == 0 else (field1_ref, 0)
         for tap_row in range(taps):
+            at = start + tap_row * SUB
             stack_ref[:, tap_row * LANES:(tap_row + 1) * LANES] = field_ref[
-                plane, tap_row * SUB:tap_row * SUB + body_rows, :
+                plane, at:at + body_rows, :
             ].astype(jnp.bfloat16)
         sides = []
         for side in range(nref):
@@ -295,19 +345,17 @@
         return value * pltpu.roll(value, SUB - 2, 1), copy
 
     halos = {}
-    ahead = min(2, planes)
-    for plane in range(ahead):
-        halos[plane] = assemble(plane)
     reductions = []
     for level in range(depth):
         total = jnp.zeros((rows, SUB, LANES), jnp.float32)
         following = {}
         for plane in range(planes):
-            halos[plane].wait()
+            if level == 0:
+                assemble(plane)
+            else:
+                halos[plane].wait()
             term, following[plane] = extrapolate(level, plane)
             total = total + term
-            if level == 0 and plane + ahead < planes:
-                halos[plane + ahead] = assemble(plane + ahead)
         halos = following
         image = jnp.sum(jnp.where(image_row, total, 0.0), axis=1)
         part_ref[:, level] = image.reshape(groups, share, LANES)
@@ -344,9 +392,13 @@
     lines = nref * 2 * taps
     members = groups * shots_axis
     scale = 1.0 / math.sqrt(planes * groups * shot_dev * shots_axis)
-    dims = (groups, shots_axis, planes, rows, own_cols, taps, nref, depth, samples)
     strips = rows * own_cols // LANES
-    packs = strips // 2 if strips % 2 == 0 else strips
+    pairs = 2 if strips % 2 == 0 else 1
+    packs = strips // pairs
+    pack_rows = pairs * (LANES // own_cols)
+    edge_packs = min(packs, -(-(taps // 2) // pack_rows))
+    margin = edge_packs * pack_rows - taps // 2
+    dims = (groups, shots_axis, planes, rows, own_cols, taps, nref, depth, samples, packs, pairs, edge_packs, margin)
     field_rows = (rows + 2 * (taps // 2)) * SUB
     share = rows // groups
     vmem = pl.BlockSpec(memory_space=pltpu.VMEM)
@@ -374,18 +426,26 @@
         ] + [
             pltpu.VMEM((groups, planes, packs * SUB, LANES), jnp.bfloat16),
             pltpu.VMEM((groups, planes, packs * SUB, LANES), jnp.bfloat16),
+            pltpu.VMEM((groups, planes, edge_packs * SUB, LANES), jnp.bfloat16),
+            pltpu.VMEM((groups, planes, edge_packs * SUB, LANES), jnp.bfloat16),
+            pltpu.VMEM(source_pattern.shape, source_pattern.dtype),
             pltpu.VMEM((lines * SEG, bin_total), jnp.bfloat16),
+            pltpu.VMEM((planes, lines * SUB, LANES), jnp.bfloat16),
             pltpu.VMEM((planes, taps * LANES, nref * 2 * LANES), jnp.bfloat16),
             pltpu.VMEM((rows * SUB, taps * LANES), jnp.bfloat16),
-            pltpu.VMEM((planes, field_rows, LANES), jnp.float32),
+            pltpu.VMEM((planes, field_rows + 2 * margin * SUB, LANES), jnp.float32),
             pltpu.VMEM((planes, field_rows, LANES), jnp.float32),
             pltpu.VMEM((groups, depth, share, LANES), jnp.float32),
             pltpu.VMEM((members, depth, share, LANES), jnp.float32),
             pltpu.SemaphoreType.DMA((len(arguments),)),
             pltpu.SemaphoreType.DMA((planes, groups)),
             pltpu.SemaphoreType.DMA((planes, groups)),
-            pltpu.SemaphoreType.DMA((depth, planes)),
-            pltpu.SemaphoreType.DMA((depth, planes)),
+            pltpu.SemaphoreType.DMA((planes, groups)),
+            pltpu.SemaphoreType.DMA((planes, groups)),
+            pltpu.SemaphoreType.DMA((1,)),
+            pltpu.SemaphoreType.DMA((1,)),
+            pltpu.SemaphoreType.DMA((depth - 1, planes)),
+            pltpu.SemaphoreType.DMA((depth - 1, planes)),
             pltpu.SemaphoreType.DMA((depth, members)),
             pltpu.SemaphoreType.DMA((depth, members)),
         ],

time: 22.3 us -> 19.7 us (0.88)
  Pallas kernels: 21.6 us -> 18.9 us
    pallas_call x1, Pallas kernels: 21.6 us -> 18.9 us  [body(): pl.pallas_call(functools.partial(kernel, dims), out_shape=jax.ShapeDtypeS...]
where the time goes in v2:
time: 19.7 us; the launch traced here: 19.6 us
  Pallas kernels  18.9 us (96%)
  other arithmetic  0.6 us (3%)
    pallas_call x1, Pallas kernels, body(): pl.pallas_call(functools.partial(kernel, dims), out_shape=jax.ShapeDtypeS...  18.9 us
    mul x1, other arithmetic, body(): return image * scale  0.6 us

profile of v2, /device:TPU:0, one launch (start us, length us, event | category | flops | bytes accessed | tf_op | source)
XLA Modules:
  0.0 19.6 jit_solution(17107742125761168528)
XLA Ops:
  0.0 18.9 %shard_map.82 = f32[1,8,2,128]{3,2,1,0:T(2,128)S(1)} custom-call(bf16[2048,512]{1,0:T(8,128)(2,1)} %bitcast.5, bf16[2,32,128]{2,1,0:T(8,128)(2,1)} %pattern_any.1, f32[2,256]{1,0:T(2,128)} %bitcast.7, bf16[26,13,2,256]{3,2,1,0:T(2,128)(2,1)} %bitcast.6, f32[64]{0:T(128)} %table_any.1, s32[2,32,128]{2,1,0:T(8,128)} %index_any.1, s32[4,6]{1,0:T(4,128)} %plan_any.1, ...), custom_call_target="tpu_custom_call" | custom-call | tf_op jit(solution)/shard_map/pallas_call | solution.py:418
  18.9 0.6 %broadcast_multiply_fusion = f32[1,8,2,128]{3,2,1,0:T(2,128)} fusion(f32[1,8,2,128]{3,2,1,0:T(2,128)S(1)} %shard_map.82), kind=kLoop, calls=%fused_computation | loop fusion | flops 2048 | bytes 16384 | tf_op jit(solution)/shard_map/mul | solution.py:456

commit v3 on v2

--- a/solution.py
+++ b/solution.py
@@ -12,6 +12,7 @@
 SUB = 8
 SEG = 16
 SLOT = 32
+CHUNKS = 2
 MESH = pl.DeviceIdType.MESH
 FPD = 3
 
@@ -21,15 +22,18 @@
     records_any, pattern_any, wavelet_any, filters_any, table_any, index_any, plan_any, counts_any,
     out_ref,
     records_ref, pattern_ref, wavelet_ref, filters_ref, table_ref, index_ref, plan_ref, counts_ref,
-    send_ref, recv_ref, edge_ref, edges_ref, beside_ref, taps_ref, lines_ref, bands_ref, stack_ref, field0_ref, field1_ref,
-    part_ref, gather_ref,
+    send_ref, recv_ref, edge_ref, edges_ref, beside_ref, taps_ref, bands_ref, field0_ref, field1_ref,
+    image_ref, part_ref, gather_ref,
     load_sem, a2a_send, a2a_recv, edge_send, edge_recv, beside_send, beside_recv, halo_send, halo_recv, red_send, red_recv,
 ):
     groups, shots_axis, planes, rows, own_cols, taps, nref, depth, samples, packs, pairs, edge_packs, margin = dims
     half_taps = taps // 2
-    pad = half_taps * SUB
-    body_rows = rows * SUB
-    slack = margin * SUB
+    pad = half_taps // 2
+    body_rows = rows // 2
+    slack = margin // 2
+    blocks_out = LANES // SLOT
+    window = LANES // 2
+    steps = (taps + 1) // 2
     freq = lax.axis_index("freq")
     shot = lax.axis_index("shot")
     half = lax.axis_index("half")
@@ -131,34 +135,32 @@
     for copy in loads[3:]:
         copy.wait()
 
-    exchanges = []
+    def drain(ref, sem):
+        pltpu.make_async_copy(ref, ref, sem).wait()
+
     for plane in range(planes):
-        arriving = []
         for step in range(1, groups):
             other = lax.rem(freq + step, groups)
             copy = pltpu.make_async_remote_copy(
                 src_ref=send_ref.at[other, plane],
                 dst_ref=recv_ref.at[freq, plane],
-                send_sem=a2a_send.at[plane, step],
-                recv_sem=a2a_recv.at[plane, step],
+                send_sem=a2a_send.at[0],
+                recv_sem=a2a_recv.at[plane],
                 device_id={"freq": other},
                 device_id_type=MESH,
             )
             copy.start()
-            arriving.append(copy)
         for step in range(groups):
             other = lax.rem(freq + step, groups)
             copy = pltpu.make_async_remote_copy(
                 src_ref=edge_ref.at[other, plane],
                 dst_ref=edges_ref.at[freq, plane],
-                send_sem=edge_send.at[plane, step],
-                recv_sem=edge_recv.at[plane, step],
+                send_sem=edge_send.at[0],
+                recv_sem=edge_recv.at[plane],
                 device_id={"freq": other, "half": 1 - half},
                 device_id_type=MESH,
             )
             copy.start()
-            arriving.append(copy)
-        exchanges.append(arriving)
     beside = pltpu.make_async_remote_copy(
         src_ref=pattern_ref,
         dst_ref=beside_ref,
@@ -175,7 +177,7 @@
     taps_ref[...] = jnp.zeros_like(taps_ref)
     for segment in range(segments):
         for tap in range(taps):
-            at = segment * 2 * SEG + 2 * tap
+            at = ((segment % taps) * nref + segment // taps) * 2 * SEG + 2 * tap
             taps_ref[at:at + 2, :] = filters_ref[segment, tap]
     bin_lane = lax.broadcasted_iota(jnp.int32, (planes * SUB, bin_total), 1)
     bin_row = lax.broadcasted_iota(jnp.int32, (planes * SUB, bin_total), 0) // SUB
@@ -194,49 +196,58 @@
         & (pick_lane % 2 == (turn_lane // SLOT) % 2)
         & ((pick_lane % (2 * SEG)) // 2 + turn_lane % SLOT == taps - 1)
     ).astype(jnp.float32).astype(jnp.bfloat16)
+    bases = [[] for _ in range(planes)]
+    per_row = nref * 2 * SEG
     for at in range(0, segments * 2 * SEG, LANES):
         width = min(LANES, segments * 2 * SEG - at)
         turned = jnp.dot(picked[:, at:at + width], turn[:width, :], preferred_element_type=jnp.float32)
-        first = at // SEG
-        for line in range(first, min(first + 2 * per_tile, 2 * segments), 2):
-            place = (line - first) * SLOT
+        for more in range(width // per_row):
             for plane in range(planes):
-                base = turned[plane * SUB:(plane + 1) * SUB, place // LANES * LANES:place // LANES * LANES + LANES]
-                shift = -(place % LANES) % LANES
-                own = pltpu.roll(base, shift, 1, stride=1, stride_axis=0)
-                after = pltpu.roll(base, (shift - SLOT) % LANES, 1, stride=1, stride_axis=0)
-                lines_ref[plane, line * SUB:(line + 2) * SUB, :] = jnp.concatenate([own, after], axis=0).astype(jnp.bfloat16)
-    spread = lax.broadcasted_iota(jnp.int32, (SLOT, LANES), 1) - lax.broadcasted_iota(jnp.int32, (SLOT, LANES), 0)
-    rest = jnp.zeros((LANES - SLOT, 2 * LANES), jnp.bfloat16)
-    placed = lines_ref[...].reshape(planes * 2 * segments * SUB, LANES)
-    for first in range(0, LANES, 2 * SUB):
+                base = turned[plane * SUB:(plane + 1) * SUB, more * LANES:(more + 1) * LANES]
+                bases[plane].append(pltpu.roll(base, 0, 1, stride=1, stride_axis=0))
+    placed = jnp.concatenate(sum(bases, []), axis=0).astype(jnp.bfloat16)
+    lane_in = lax.broadcasted_iota(jnp.int32, (LANES, LANES), 0)
+    lane_out = lax.broadcasted_iota(jnp.int32, (LANES, LANES), 1)
+    spread = jnp.where(lane_in // SLOT == lane_out // SLOT, lane_out - lane_in, 2 * LANES)
+    bands_ref[...] = jnp.zeros_like(bands_ref)
+    for first in range(0, SLOT + taps - 1, 2 * SUB):
         moves = jnp.concatenate(
-            [(spread == first + more - half_taps).astype(jnp.float32) for more in (0, SUB)], axis=1
+            [(spread == first + more - taps + 1).astype(jnp.float32) for more in (0, SUB)], axis=1
         ).astype(jnp.bfloat16)
-        block = jnp.dot(placed, jnp.concatenate([moves, rest], axis=0), preferred_element_type=jnp.float32)
+        block = jnp.dot(placed, moves, preferred_element_type=jnp.float32)
         for plane in range(planes):
-            for line in range(2 * segments):
-                segment = line // 2
-                at = (segment % taps) * LANES + first
-                side = (segment // taps) * 2 + line % 2
-                start = (plane * 2 * segments + line) * SUB
-                bands_ref[plane, at:at + 2 * SUB, side * LANES:(side + 1) * LANES] = jnp.concatenate(
+            for tap_row in range(taps):
+                start = (plane * taps + tap_row) * SUB
+                piece = jnp.concatenate(
                     [block[start:start + SUB, :LANES], block[start:start + SUB, LANES:]], axis=0
                 ).astype(jnp.bfloat16)
-
+                for odd in range(2):
+                    at = (tap_row + odd) * window + first
+                    bands_ref[plane, at:at + 2 * SUB, odd * LANES:(odd + 1) * LANES] = piece
+
+    slot = lax.broadcasted_iota(jnp.int32, (body_rows, LANES), 1) // SLOT
     blends = []
     for level in range(depth):
-        classes = index_ref[level]
-        weight = jnp.zeros(classes.shape, jnp.float32)
-        for entry in range(table_ref.shape[0]):
-            weight = jnp.where(classes == entry, table_ref[entry], weight)
-        blends.append(weight)
-
-    outer = pl.multiple_of(half * (body_rows + pad), SUB)
-    outer0 = pl.multiple_of(slack + half * (body_rows + pad), SUB)
+        by_parity = []
+        for odd in range(2):
+            classes = index_ref[level, pl.ds(odd, body_rows, stride=2), :]
+            weight = jnp.zeros(classes.shape, jnp.float32)
+            for entry in range(table_ref.shape[0]):
+                weight = jnp.where(classes == entry, table_ref[entry], weight)
+            wide = []
+            for place in range(blocks_out):
+                own = jnp.where(slot == place, weight, 0.0)
+                own = own + pltpu.roll(own, SLOT, 1)
+                own = own + pltpu.roll(own, window, 1)
+                wide.append(jnp.where(slot < 2, 1.0 - own, own))
+            by_parity.append(wide)
+        blends.append(by_parity)
+
+    outer = half * (body_rows + pad)
     for plane in range(planes):
-        field0_ref[plane, pl.ds(outer0, pad), :] = jnp.zeros((pad, LANES), jnp.float32)
-        field1_ref[plane, pl.ds(outer, pad), :] = jnp.zeros((pad, LANES), jnp.float32)
+        blank = jnp.zeros((pad, blocks_out * SUB, LANES), jnp.bfloat16)
+        field0_ref[plane, pl.ds(slack + outer, pad)] = blank
+        field1_ref[plane, pl.ds(outer, pad)] = blank
     pattern = [pattern_ref[index].astype(jnp.float32) for index in range(2)]
     wave_lane = lax.broadcasted_iota(jnp.int32, wavelet_ref.shape, 1)
     gains = []
@@ -252,14 +263,14 @@
             )
         )
 
-    inner = pl.multiple_of(body_rows - half * (body_rows - pad), SUB)
-    target = pl.multiple_of(half * (body_rows + pad), SUB)
+    inner = body_rows - half * (body_rows - pad)
+    target = half * (body_rows + pad)
 
     def swap(level, plane):
         field_ref = field1_ref
         copy = pltpu.make_async_remote_copy(
-            src_ref=field_ref.at[plane, pl.ds(inner, pad), :],
-            dst_ref=field_ref.at[plane, pl.ds(target, pad), :],
+            src_ref=field_ref.at[plane, pl.ds(inner, pad)],
+            dst_ref=field_ref.at[plane, pl.ds(target, pad)],
             send_sem=halo_send.at[level - 1, plane],
             recv_sem=halo_recv.at[level - 1, plane],
             device_id={"half": 1 - half},
@@ -270,16 +281,33 @@
 
     strip_rows = LANES // own_cols
     edge_rows = edge_packs * pairs * strip_rows
-    edge_at = pl.multiple_of(
-        jnp.where(half == 0, slack + pad + body_rows, slack + pad - edge_rows * SUB), SUB
-    )
+    edge_at = jnp.where(half == 0, slack + pad + body_rows, slack + pad - edge_rows // 2)
     beside.wait()
     besides = []
     for index in range(2):
         other_half = beside_ref[index].astype(jnp.float32)
         besides.append(jnp.where(half == 0, other_half[:edge_rows, :], other_half[rows - edge_rows:, :]))
 
-    def unfold(blocks, count, patterns, plane, put):
+    def windows(even, odd):
+        lane3 = lax.broadcasted_iota(jnp.int32, even.shape, 2)
+        side = lane3 % window
+        turned = []
+        for place in range(blocks_out):
+            start = place * SLOT - half_taps
+            seen = jnp.where(
+                lane3 < window,
+                pltpu.roll(even, -start % LANES, 2),
+                pltpu.roll(odd, (window - start) % LANES, 2),
+            )
+            if start < 0:
+                seen = jnp.where(side < -start, 0.0, seen)
+            if start + SLOT + taps - 1 > LANES:
+                seen = jnp.where(side >= LANES - start, 0.0, seen)
+            turned.append(seen)
+        return jnp.concatenate(turned, axis=1).astype(jnp.bfloat16)
+
+    def unfold(blocks, count, patterns, plane):
+        found = {}
         lane = lax.broadcasted_iota(jnp.int32, (count * SUB, LANES), 1) // own_cols
         for low in range(strip_rows):
             merged = jnp.zeros((count * SUB, LANES), jnp.float32)
@@ -298,82 +326,124 @@
                         odd_shot, patterns[1][row:row + 1, :], patterns[0][row:row + 1, :]
                     ) * gains[plane]
                     source = source.astype(jnp.bfloat16).astype(jnp.float32)
-                    put(row, jnp.where(second, receiver, source))
+                    found[row] = jnp.where(second, receiver, source)
+        return windows(
+            jnp.stack([found[row] for row in range(0, len(found), 2)]),
+            jnp.stack([found[row] for row in range(1, len(found), 2)]),
+        )
+
+    def arrive(plane):
+        drain(recv_ref.at[pl.ds(0, groups - 1), plane], a2a_recv.at[plane])
+        drain(edges_ref.at[:, plane], edge_recv.at[plane])
 
     def assemble(plane):
-        for copy in exchanges[plane]:
-            copy.wait()
-
-        def put_body(row, value):
-            at = slack + pad + row * SUB
-            field0_ref[plane, at:at + SUB, :] = value
-
-        def put_edge(row, value):
-            field0_ref[plane, pl.ds(pl.multiple_of(edge_at + row * SUB, SUB), SUB), :] = value
-
-        unfold([recv_ref[group, plane].astype(jnp.float32) for group in range(groups)], packs, pattern, plane, put_body)
-        unfold([edges_ref[group, plane].astype(jnp.float32) for group in range(groups)], edge_packs, besides, plane, put_edge)
-
-    row3 = lax.broadcasted_iota(jnp.int32, (rows, SUB, LANES), 1)
-    sign = jnp.where(row3 >= SUB // 2, 1.0, -1.0)
+        blocks = [recv_ref[group, plane].astype(jnp.float32) for group in range(groups)]
+        edges = [edges_ref[group, plane].astype(jnp.float32) for group in range(groups)]
+        field0_ref[plane, slack + pad:slack + pad + body_rows] = unfold(blocks, packs, pattern, plane)
+        field0_ref[plane, pl.ds(edge_at, edge_rows // 2)] = unfold(edges, edge_packs, besides, plane)
+
+    part_shape = (body_rows // CHUNKS, SUB, LANES)
+    row3 = lax.broadcasted_iota(jnp.int32, (body_rows, SUB, LANES), 1)
+    slot3 = lax.broadcasted_iota(jnp.int32, part_shape, 2) // SLOT
+    low3 = slot3 < 2
+    middle3 = (slot3 == 1) | (slot3 == 2)
+    even3 = slot3 % 2 == 0
+    sign = jnp.where(lax.broadcasted_iota(jnp.int32, part_shape, 1) >= SUB // 2, 1.0, -1.0)
     image_row = (row3 & 2) == 0
     share = rows // groups
 
-    def extrapolate(level, plane):
+    def cross(value):
+        return sign * pltpu.roll(value, SUB // 2, 1)
+
+    def multiply(level, plane):
         field_ref, start = (field0_ref, slack) if level == 0 else (field1_ref, 0)
-        for tap_row in range(taps):
-            at = start + tap_row * SUB
-            stack_ref[:, tap_row * LANES:(tap_row + 1) * LANES] = field_ref[
-                plane, at:at + body_rows, :
-            ].astype(jnp.bfloat16)
-        sides = []
-        for side in range(nref):
-            both = jnp.dot(
-                stack_ref[...],
-                bands_ref[plane, :, 2 * side * LANES:2 * (side + 1) * LANES],
-                preferred_element_type=jnp.float32,
-            )
-            direct = both[:, :LANES].reshape(rows, SUB, LANES)
-            crossed = both[:, LANES:].reshape(rows, SUB, LANES)
-            sides.append(direct + sign * pltpu.roll(crossed, SUB // 2, 1))
-        value = sides[0] + blends[level][:, None, :] * (sides[1] - sides[0])
-        value = value.astype(jnp.bfloat16).astype(jnp.float32)
+        chunk = body_rows // CHUNKS
+        products = []
+        for at in range(start, start + body_rows, chunk):
+            seen = jnp.concatenate(
+                [
+                    field_ref[plane, at + step:at + step + chunk].reshape(chunk * blocks_out * SUB, LANES)
+                    for step in range(steps)
+                ],
+                axis=1,
+            )
+            products.append(jnp.dot(seen, bands_ref[plane], preferred_element_type=jnp.float32))
+        return products
+
+    def finish(level, plane, products):
+        chunk = body_rows // CHUNKS
+        parts = [[], []]
+        for index, both in enumerate(products):
+            both = both.reshape(chunk, blocks_out, SUB, 2 * LANES)
+            for odd in range(2):
+                z = [
+                    both[:, place, :, odd * LANES:(odd + 1) * LANES]
+                    * blends[level][odd][place][index * chunk:(index + 1) * chunk][:, None, :]
+                    for place in range(blocks_out)
+                ]
+                first = jnp.where(low3, z[0], z[2]) + pltpu.roll(jnp.where(low3, z[2], z[0]), window, 2)
+                after = jnp.where(middle3, z[1], z[3]) + pltpu.roll(jnp.where(middle3, z[3], z[1]), window, 2)
+                value = jnp.where(even3, first, cross(after)) + pltpu.roll(
+                    jnp.where(even3, after, cross(first)), LANES - SLOT, 2
+                )
+                parts[odd].append(value.astype(jnp.bfloat16).astype(jnp.float32))
+        values = [jnp.concatenate(part, axis=0) for part in parts]
         copy = None
         if level + 1 < depth:
-            field1_ref[plane, pad:pad + body_rows, :] = value.reshape(body_rows, LANES)
+            field1_ref[plane, pad:pad + body_rows] = windows(*values)
             copy = swap(level + 1, plane)
-        return value * pltpu.roll(value, SUB - 2, 1), copy
+        return [value * pltpu.roll(value, SUB - 2, 1) for value in values], copy
 
     halos = {}
-    reductions = []
-    for level in range(depth):
-        total = jnp.zeros((rows, SUB, LANES), jnp.float32)
-        following = {}
-        for plane in range(planes):
-            if level == 0:
-                assemble(plane)
-            else:
-                halos[plane].wait()
-            term, following[plane] = extrapolate(level, plane)
-            total = total + term
-        halos = following
-        image = jnp.sum(jnp.where(image_row, total, 0.0), axis=1)
+    totals = {}
+
+    def settle(level, plane, products):
+        terms, halos[level + 1, plane] = finish(level, plane, products)
+        if plane:
+            terms = [total + term for total, term in zip(totals[level], terms)]
+        totals[level] = terms
+        if plane + 1 == planes:
+            reduce(level)
+
+    def reduce(level):
+        for odd in range(2):
+            image_ref[pl.ds(odd, body_rows, stride=2), :] = jnp.sum(
+                jnp.where(image_row, totals[level][odd], 0.0), axis=1
+            )
+        image = image_ref[...]
         part_ref[:, level] = image.reshape(groups, share, LANES)
         for step in range(1, members):
             other = lax.rem(me + step, members)
             copy = pltpu.make_async_remote_copy(
                 src_ref=part_ref.at[other // shots_axis, level],
                 dst_ref=gather_ref.at[me, level],
-                send_sem=red_send.at[level, step],
-                recv_sem=red_recv.at[level, step],
+                send_sem=red_send.at[0],
+                recv_sem=red_recv.at[0],
                 device_id={"freq": other // shots_axis, "shot": lax.rem(other, shots_axis)},
                 device_id_type=MESH,
             )
             copy.start()
-            reductions.append(copy)
+    arrive(0)
+    assemble(0)
+    for plane in range(1, planes):
+        arrive(plane)
+    waiting = None
+    for level in range(depth):
+        for plane in range(planes):
+            if level:
+                halos[level, plane].wait()
+            elif plane:
+                assemble(plane)
+            products = multiply(level, plane)
+            if waiting is not None:
+                settle(*waiting)
+            waiting = (level, plane, products)
+    settle(*waiting)
     gather_ref[me] = part_ref[freq]
-    for copy in reductions:
-        copy.wait()
+    drain(gather_ref.at[pl.ds(0, members - 1)], red_recv.at[0])
+    drain(gather_ref.at[pl.ds(0, members - 1)], red_send.at[0])
+    drain(send_ref.at[pl.ds(0, groups - 1)], a2a_send.at[0])
+    drain(edge_ref, edge_send.at[0])
     result = gather_ref[0]
     for index in range(1, members):
         result = result + gather_ref[index]
@@ -399,7 +469,7 @@
     edge_packs = min(packs, -(-(taps // 2) // pack_rows))
     margin = edge_packs * pack_rows - taps // 2
     dims = (groups, shots_axis, planes, rows, own_cols, taps, nref, depth, samples, packs, pairs, edge_packs, margin)
-    field_rows = (rows + 2 * (taps // 2)) * SUB
+    row_pairs = rows // 2 + taps // 2
     share = rows // groups
     vmem = pl.BlockSpec(memory_space=pltpu.VMEM)
     anywhere = pl.BlockSpec(memory_space=pltpu.HBM)
@@ -430,24 +500,23 @@
             pltpu.VMEM((groups, planes, edge_packs * SUB, LANES), jnp.bfloat16),
             pltpu.VMEM(source_pattern.shape, source_pattern.dtype),
             pltpu.VMEM((lines * SEG, bin_total), jnp.bfloat16),
-            pltpu.VMEM((planes, lines * SUB, LANES), jnp.bfloat16),
-            pltpu.VMEM((planes, taps * LANES, nref * 2 * LANES), jnp.bfloat16),
-            pltpu.VMEM((rows * SUB, taps * LANES), jnp.bfloat16),
-            pltpu.VMEM((planes, field_rows + 2 * margin * SUB, LANES), jnp.float32),
-            pltpu.VMEM((planes, field_rows, LANES), jnp.float32),
+            pltpu.VMEM((planes, (taps + 1) // 2 * LANES, 2 * LANES), jnp.bfloat16),
+            pltpu.VMEM((planes, row_pairs + margin, LANES // SLOT * SUB, LANES), jnp.bfloat16),
+            pltpu.VMEM((planes, row_pairs, LANES // SLOT * SUB, LANES), jnp.bfloat16),
+            pltpu.VMEM((rows, LANES), jnp.float32),
             pltpu.VMEM((groups, depth, share, LANES), jnp.float32),
             pltpu.VMEM((members, depth, share, LANES), jnp.float32),
             pltpu.SemaphoreType.DMA((len(arguments),)),
-            pltpu.SemaphoreType.DMA((planes, groups)),
-            pltpu.SemaphoreType.DMA((planes, groups)),
-            pltpu.SemaphoreType.DMA((planes, groups)),
-            pltpu.SemaphoreType.DMA((planes, groups)),
+            pltpu.SemaphoreType.DMA((1,)),
+            pltpu.SemaphoreType.DMA((planes,)),
+            pltpu.SemaphoreType.DMA((1,)),
+            pltpu.SemaphoreType.DMA((planes,)),
             pltpu.SemaphoreType.DMA((1,)),
             pltpu.SemaphoreType.DMA((1,)),
             pltpu.SemaphoreType.DMA((depth - 1, planes)),
             pltpu.SemaphoreType.DMA((depth - 1, planes)),
-            pltpu.SemaphoreType.DMA((depth, members)),
-            pltpu.SemaphoreType.DMA((depth, members)),
+            pltpu.SemaphoreType.DMA((1,)),
+            pltpu.SemaphoreType.DMA((1,)),
         ],
         compiler_params=pltpu.CompilerParams(
             collective_id=0, has_side_effects=True, vmem_limit_bytes=24 << 20

time: 19.7 us -> 19 us (0.964)
  Pallas kernels: 18.9 us -> 18.2 us
    pallas_call x1, Pallas kernels: 18.9 us -> 18.2 us  [body(): pl.pallas_call(functools.partial(kernel, dims), out_shape=jax.ShapeDtypeS...]
where the time goes in v3:
time: 19 us; the launch traced here: 18.8 us
  Pallas kernels  18.2 us (96%)
  other arithmetic  0.6 us (3%)
    pallas_call x1, Pallas kernels, body(): pl.pallas_call(functools.partial(kernel, dims), out_shape=jax.ShapeDtypeS...  18.2 us
    mul x1, other arithmetic, body(): return image * scale  0.6 us

profile of v3, /device:TPU:0, one launch (start us, length us, event | category | flops | bytes accessed | tf_op | source)
XLA Modules:
  0.0 18.8 jit_solution(11090363271541987510)
XLA Ops:
  0.0 18.2 %shard_map.82 = f32[1,8,2,128]{3,2,1,0:T(2,128)S(1)} custom-call(bf16[2048,512]{1,0:T(8,128)(2,1)} %bitcast.5, bf16[2,32,128]{2,1,0:T(8,128)(2,1)} %pattern_any.1, f32[2,256]{1,0:T(2,128)} %bitcast.7, bf16[26,13,2,256]{3,2,1,0:T(2,128)(2,1)} %bitcast.6, f32[64]{0:T(128)} %table_any.1, s32[2,32,128]{2,1,0:T(8,128)} %index_any.1, s32[4,6]{1,0:T(4,128)} %plan_any.1, ...), custom_call_target="tpu_custom_call" | custom-call | tf_op jit(solution)/shard_map/pallas_call | solution.py:488
  18.2 0.6 %broadcast_multiply_fusion = f32[1,8,2,128]{3,2,1,0:T(2,128)} fusion(f32[1,8,2,128]{3,2,1,0:T(2,128)S(1)} %shard_map.82), kind=kLoop, calls=%fused_computation | loop fusion | flops 2048 | bytes 16384 | tf_op jit(solution)/shard_map/mul | solution.py:525
